TPU v7x, 32 devices: a whole 2x2x4 slice. The times are simulated.
32 devices in a mesh: expert: 4 (over z), dp: 8 (over y, x, core).
Axes of the slice: x: 2, y: 2, z: 4, core: 2. Of those that a mesh axis runs over, the one named last changes fastest.
Arguments:
- grad_out: bfloat16 [4096, 2048], P(('expert', 'dp')), may hold values from -1.59375 to 1.59375
- slot_token: int32 [32, 8, 8], P(('expert', 'dp')), may hold values from 0 to 127, as said below
- hidden: bfloat16 [2048, 768], P(('expert', 'dp')), may hold values from -6 to 6
- slot_weight: float32 [32, 64], P(('expert', 'dp')), may hold values from 0.05 to 0.5
- counts: int32 [32, 8], P(('expert', 'dp')), may hold values from 0 to 8, as said below
- master_weight: bfloat16 [8, 768, 2048], P('expert', 'dp')
- moment1: bfloat16 [8, 768, 2048], P('expert', 'dp')
- moment2: bfloat16 [8, 768, 2048], P('expert', 'dp'), may hold values from 0.099609375 to 2
Outputs:
- new_weight: bfloat16 [8, 768, 2048], P('expert', 'dp')
Inputs may be any that keep to these rules, and one draw needn't show every extreme that they name: `slot_token`: within one device's block for one expert, the 8 slots name different tokens. `counts`: in every draw some expert has 8 live slots from every device.
All inputs are finite; a program needn't handle non-finite values.
Results may differ from a plain program's by a relative error of at most 0.0055.
Values may be sent and summed in bfloat16 or wider, within the bound.
A program may use at most 64 MiB of HBM per device.

v0:
```python
import jax
import jax.numpy as jnp
from jax import lax
from jax.sharding import PartitionSpec as P

learn_rate = 0.3
decay_rate = 0.01
adam_eps = 1e-06
norm_eps = 1e-06
bias_one = 1.0 - 0.9**10
bias_two = 1.0 - 0.999**10


def local(grad_out, slot_token, hidden, slot_weight, counts, master_weight, moment1, moment2):
    n_expert = lax.axis_size("expert")
    experts_here = master_weight.shape[0]
    capacity = slot_token.shape[2]
    width = grad_out.shape[1]
    depth = hidden.shape[1]
    weight = master_weight.astype(jnp.float32)
    first = moment1.astype(jnp.float32)
    second = moment2.astype(jnp.float32)
    weight_sq = jnp.sum(weight * weight, axis=(1, 2))
    weight_total = lax.psum(weight_sq, "dp")
    picked = jnp.take(grad_out, slot_token.reshape(-1), axis=0).reshape(
        n_expert, experts_here * capacity, width
    )
    arrived = lax.all_to_all(picked, "expert", split_axis=0, concat_axis=0, tiled=True)
    arrived = arrived.reshape(n_expert, experts_here, capacity, width)
    slot_ids = lax.broadcasted_iota(jnp.int32, (n_expert, experts_here, capacity), 2)
    is_live = slot_ids < counts.reshape(n_expert, experts_here)[:, :, None]
    mixing = jnp.where(is_live, slot_weight.reshape(n_expert, experts_here, capacity), 0.0).astype(
        jnp.bfloat16
    )
    scaled = (mixing.astype(jnp.float32)[..., None] * arrived.astype(jnp.float32)).astype(
        jnp.bfloat16
    )
    saved = hidden.reshape(n_expert, experts_here, capacity, depth)
    shares = []
    for j in range(experts_here):
        saved_rows = saved[:, j].reshape(-1, depth)
        scaled_rows = scaled[:, j].reshape(-1, width)
        term = jnp.dot(saved_rows.T, scaled_rows, preferred_element_type=jnp.float32)
        shares.append(
            lax.psum_scatter(
                term.astype(jnp.bfloat16).astype(jnp.float32).astype(jnp.bfloat16),
                "dp",
                scatter_dimension=0,
                tiled=True,
            ).astype(jnp.float32)
        )
    gradient = jnp.stack(shares)
    first_new = 0.9 * first + 0.1 * gradient
    second_new = 0.999 * second + 0.001 * gradient * gradient
    update = (
        first_new / bias_one / (jnp.sqrt(second_new / bias_two) + adam_eps) + decay_rate * weight
    )
    update_sq = jnp.sum(update * update, axis=(1, 2))
    update_total = lax.psum(update_sq, "dp")
    trust_ratio = jnp.sqrt(weight_total) / (jnp.sqrt(update_total) + norm_eps)
    fresh = weight - learn_rate * trust_ratio[:, None, None] * update
    return fresh.astype(jnp.bfloat16)


def solution(mesh):
    placed = (
        P(("expert", "dp"), None),
        P(("expert", "dp"), None, None),
        P(("expert", "dp"), None),
        P(("expert", "dp"), None),
        P(("expert", "dp"), None),
        P("expert", "dp", None),
        P("expert", "dp", None),
        P("expert", "dp", None),
    )
    return jax.shard_map(
        local, mesh=mesh, in_specs=placed, out_specs=P("expert", "dp", None), check_vma=False
    )
```

profile of v0, /device:TPU:0, one launch (start us, length us, event | category | flops | bytes accessed | tf_op | source)
XLA Modules:
  0.0 151.3 jit_solution(233067076570586812)
XLA Ops:
  6.5 0.0 copy-start
  6.5 0.8 reshape.83
  7.4 0.8 reshape.82
  8.2 0.0 copy-done
  8.2 0.0 copy-start.3
  8.2 0.0 copy-start.4
  8.2 0.0 copy-start.2
  8.2 0.7 gather_fusion
  8.9 0.8 broadcast_select_fusion
  9.7 6.3 %all-to-all-start = ((bf16[4,16,2048]{2,1,0:T(8,128)(2,1)}), bf16[4,16,2048]{2,1,0:T(8,128)(2,1)S(1)}, u32[]{:S(2)}, u32[]{:S(2)}) async-start(bf16[4,16,2048]{2,1,0:T(8,128)(2,1)} %broadcast_select_fusion), calls=%async_computation | async-start | bytes 524288 | tf_op jit(solution)/shard_map/all_to_all | solution.py:28
  16.1 0.0 reduce-scatter.9.cloned.1.call-start
  16.1 0.6 broadcast.63
  16.7 0.0 copy-done.3
  16.7 0.7 reduce.6
  17.4 0.1 reshape.81
  17.5 0.6 broadcast.64
  18.1 0.0 copy-done.4
  18.1 0.7 reduce.7
  18.8 0.1 lt.36
  18.9 0.1 fusion.14
  19.0 6.0 %all-to-all-done = bf16[4,16,2048]{2,1,0:T(8,128)(2,1)S(1)} async-done(((bf16[4,16,2048]{2,1,0:T(8,128)(2,1)}), bf16[4,16,2048]{2,1,0:T(8,128)(2,1)S(1)}, u32[]{:S(2)}, u32[]{:S(2)}) %all-to-all-start) | async-done | bytes 262176 | tf_op jit(solution)/shard_map/all_to_all | solution.py:28
  25.0 0.1 fusion.12
  25.1 0.0 copy-done.2
  25.1 2.7 %fusion.1 = bf16[768,2048]{0,1:T(8,128)(2,1)} fusion(bf16[4,2,8,2048]{3,2,0,1:T(8,128)(2,1)S(1)} %fusion.12, bf16[4,2,8,768]{3,2,1,0:T(8,128)(2,1)S(1)} %bitcast.43), kind=kOutput, calls=%fused_computation.4 | convolution fusion | flops 102236160 | bytes 3325952 | tf_op jit(solution)/shard_map/dot_general | solution.py:43
  27.9 4.8 %copy.38 = bf16[768,2048]{1,0:T(8,128)(2,1)} copy(bf16[768,2048]{0,1:T(8,128)(2,1)} %fusion.1) | data formatting | bytes 6291456
  32.6 0.0 reduce-scatter.9.cloned.1.call-update
  32.6 0.0 reduce-scatter.7.cloned.1.call-start
  32.7 2.7 %fusion = bf16[768,2048]{0,1:T(8,128)(2,1)} fusion(bf16[4,2,8,2048]{3,2,0,1:T(8,128)(2,1)S(1)} %fusion.12, bf16[4,2,8,768]{3,2,1,0:T(8,128)(2,1)S(1)} %bitcast.44), kind=kOutput, calls=%fused_computation.3 | convolution fusion | flops 102236160 | bytes 3325952 | tf_op jit(solution)/shard_map/dot_general | solution.py:43
  35.4 4.7 %copy.36 = bf16[768,2048]{1,0:T(8,128)(2,1)} copy(bf16[768,2048]{0,1:T(8,128)(2,1)} %fusion) | data formatting | bytes 6291456
  40.2 0.0 copy-start.1
  40.2 0.0 reduce-scatter.7.cloned.1.call-update
  40.2 37.7 %reduce-scatter.9.cloned.1.call-done = bf16[96,2048]{1,0:T(8,128)(2,1)} async-done(((bf16[768,2048]{1,0:T(8,128)(2,1)}), bf16[96,2048]{1,0:T(8,128)(2,1)}) %reduce-scatter.9.cloned.1.call-update) | async-done | bytes 393232 | tf_op jit(solution)/shard_map/reduce_scatter | solution.py:45
  77.9 49.5 %reduce-scatter.7.cloned.1.call-done = bf16[96,2048]{1,0:T(8,128)(2,1)} async-done(((bf16[768,2048]{1,0:T(8,128)(2,1)}), bf16[96,2048]{1,0:T(8,128)(2,1)}) %reduce-scatter.7.cloned.1.call-update) | async-done | bytes 393232 | tf_op jit(solution)/shard_map/reduce_scatter | solution.py:45
  127.4 0.0 copy-done.1
  127.4 3.4 %multiply_reduce_fusion = (f32[2]{0:T(128)S(1)}, f32[2,96,2048]{2,1,0:T(8,128)S(1)}, f32[2]{0:T(128)S(1)}) fusion(bf16[2,96,2048]{2,1,0:T(8,128)(2,1)S(1)} %copy-done.1, bf16[2,96,2048]{2,1,0:T(8,128)(2,1)} %param.15, bf16[1,96,2048]{2,1,0:T(8,128)(2,1)} %bitcast.41, bf16[1,96,2048]{2,1,0:T(8,128)(2,1)} %bitcast.42, bf16[2,96,2048]{2,1,0:T(8,128)(2,1)} %param.14), kind=kLoop, calls=%fused_computation.20 | loop fusion | flops 8650748 | bytes 4718608 | tf_op jit(solution)/shard_map/reduce_sum | solution.py:58
  130.8 12.5 %all-reduce = (f32[2]{0:T(128)S(1)}, f32[2]{0:T(128)S(1)}) all-reduce(f32[2]{0:T(128)S(1)} %get-tuple-element.7, f32[2]{0:T(128)S(1)} %get-tuple-element.9), channel_id=1, replica_groups=mesh['expert'=4,'dp'=8] {'dp'}, use_global_device_ids=true, to_apply=%region_5.6 | all-reduce | flops 4 | bytes 32 | tf_op jit(solution)/shard_map/psum | solution.py:59
  143.3 1.2 fusion.7
  (5 shorter events, 0.0 us)
Async XLA Ops:
  6.5 1.6 %copy-start = (bf16[128,2048]{1,0:T(8,128)(2,1)S(1)}, bf16[128,2048]{1,0:T(8,128)(2,1)}, u32[]{:S(2)}) copy-start(bf16[128,2048]{1,0:T(8,128)(2,1)} %param.8) | copy-start | bytes 1572868
  8.2 8.5 %copy-start.3 = (f32[1,64]{1,0:T(1,128)S(1)}, f32[1,64]{1,0:T(1,128)}, u32[]{:S(2)}) copy-start(f32[1,64]{1,0:T(1,128)} %param.11) | copy-start | bytes 772
  8.2 9.9 %copy-start.4 = (s32[1,8]{1,0:T(1,128)S(1)}, s32[1,8]{1,0:T(1,128)}, u32[]{:S(2)}) copy-start(s32[1,8]{1,0:T(1,128)} %param.12) | copy-start | bytes 100
  8.2 16.9 %copy-start.2 = (bf16[64,768]{1,0:T(8,128)(2,1)S(1)}, bf16[64,768]{1,0:T(8,128)(2,1)}, u32[]{:S(2)}) copy-start(bf16[64,768]{1,0:T(8,128)(2,1)} %param.10) | copy-start | bytes 294916
  9.7 15.3 %all-to-all-start = ((bf16[4,16,2048]{2,1,0:T(8,128)(2,1)}), bf16[4,16,2048]{2,1,0:T(8,128)(2,1)S(1)}, u32[]{:S(2)}, u32[]{:S(2)}) async-start(bf16[4,16,2048]{2,1,0:T(8,128)(2,1)} %broadcast_select_fusion), calls=%async_computation | async-start | bytes 524288 | tf_op jit(solution)/shard_map/all_to_all | solution.py:28
  16.1 61.8 %reduce-scatter.9.cloned.1.call-start = ((), (), s32[]{:S(2)}) async-start(), calls=%async_computation.4 | async-start | bytes 3538944 | tf_op jit(solution)/shard_map/reduce_scatter | solution.py:45
  32.6 94.7 %reduce-scatter.7.cloned.1.call-start = ((), (), s32[]{:S(2)}) async-start(), calls=%async_computation.3 | async-start | bytes 3538944 | tf_op jit(solution)/shard_map/reduce_scatter | solution.py:45
  40.2 87.2 %copy-start.1 = (bf16[2,96,2048]{2,1,0:T(8,128)(2,1)S(1)}, bf16[2,96,2048]{2,1,0:T(8,128)(2,1)}, u32[]{:S(2)}) copy-start(bf16[2,96,2048]{2,1,0:T(8,128)(2,1)} %param.13) | copy-start | bytes 2359300
Sparse Core Ops, SparseCore 0:
  32.8 45.1 reduce-scatter.8
  81.3 46.0 reduce-scatter.6
where the time goes:
time: 152 us; the launch traced here: 151 us
  waiting for transfers between devices  93.3 us (61%)
  between operations  13.5 us (9%)
  local copies, waits for them, and re-layouts  13.2 us (9%)
  blocking collectives  12.5 us (8%)
  other arithmetic  6.99 us (5%)
  starting transfers between devices  6.39 us (4%)
  matrix products  5.46 us (4%)
    reduce_scatter x2, waiting for transfers between devices, local(): lax.psum_scatter(term.astype(jnp.bfloat16).astype(jnp.float32).astype(jnp...  87.2 us
    psum x1, blocking collectives, local(): update_total = lax.psum(update_sq, 'dp')  12.5 us
    unnamed x14, local copies, waits for them, and re-layouts  10.7 us
    all_to_all x1, starting transfers between devices, local(): lax.all_to_all(picked, 'expert', split_axis=0, concat_axis=0, tiled=True)  6.35 us
    all_to_all x1, waiting for transfers between devices, local(): lax.all_to_all(picked, 'expert', split_axis=0, concat_axis=0, tiled=True)  6.05 us
    dot_general x2, matrix products, local(): jnp.dot(saved_rows.T, scaled_rows, preferred_element_type=jnp.float32)  5.46 us
    reduce_sum x1, other arithmetic, local(): update_sq = jnp.sum(update * update, axis=(1, 2))  3.4 us
  transfers between devices with their start and end apart: 3, of which 3 were waited for; matrix products, arithmetic and copies ran while one was open for 7% of the time, Pallas kernels for 0%

commit v1 on v0

--- a/solution.py
+++ b/solution.py
@@ -9,6 +9,14 @@
 norm_eps = 1e-06
 bias_one = 1.0 - 0.9**10
 bias_two = 1.0 - 0.999**10
+
+
+def added_up(shard, axis):
+    n_dev, acc = (lax.axis_size(axis), shard)
+    for far in [1 << k for k in range(n_dev.bit_length() - 1)]:
+        pairs = [(i, i ^ far) for i in range(n_dev)]
+        acc = acc + lax.ppermute(acc, axis, pairs)
+    return acc
 
 
 def local(grad_out, slot_token, hidden, slot_weight, counts, master_weight, moment1, moment2):
@@ -56,7 +64,7 @@
         first_new / bias_one / (jnp.sqrt(second_new / bias_two) + adam_eps) + decay_rate * weight
     )
     update_sq = jnp.sum(update * update, axis=(1, 2))
-    update_total = lax.psum(update_sq, "dp")
+    update_total = added_up(update_sq, "dp")
     trust_ratio = jnp.sqrt(weight_total) / (jnp.sqrt(update_total) + norm_eps)
     fresh = weight - learn_rate * trust_ratio[:, None, None] * update
     return fresh.astype(jnp.bfloat16)

time: 152 us -> 160 us (1.053)
  waiting for transfers between devices: 93.3 us -> 100 us
    ppermute x0 -> x3, waiting for transfers between devices: none -> 6.83 us  [added_up(): acc = acc + lax.ppermute(acc, axis, pairs)]
  transfers between devices with their start and end apart: 3 -> 6, of which waited for: 3 -> 6; matrix products, arithmetic and copies ran while one was open for 7% -> 6% of each run, Pallas kernels for 0% -> 0%
where the time goes in v1:
time: 160 us
  waiting for transfers between devices  100 us (62%)
  between operations  13.5 us (8%)
  local copies, waits for them, and re-layouts  13.2 us (8%)
  blocking collectives  12.5 us (8%)
  starting transfers between devices  7.9 us (5%)
  other arithmetic  6.99 us (4%)
  matrix products  5.46 us (3%)
    reduce_scatter x2, waiting for transfers between devices, local(): lax.psum_scatter(term.astype(jnp.bfloat16).astype(jnp.float32).astype(jnp...  87.2 us
    psum x1, blocking collectives, local(): weight_total = lax.psum(weight_sq, 'dp')  12.5 us
    unnamed x14, local copies, waits for them, and re-layouts  10.7 us
    ppermute x3, waiting for transfers between devices, added_up(): acc = acc + lax.ppermute(acc, axis, pairs)  6.83 us
    all_to_all x1, starting transfers between devices, local(): lax.all_to_all(picked, 'expert', split_axis=0, concat_axis=0, tiled=True)  6.35 us
    all_to_all x1, waiting for transfers between devices, local(): lax.all_to_all(picked, 'expert', split_axis=0, concat_axis=0, tiled=True)  6.05 us
    dot_general x2, matrix products, local(): jnp.dot(saved_rows.T, scaled_rows, preferred_element_type=jnp.float32)  5.46 us
    reduce_sum x1, other arithmetic, local(): update_sq = jnp.sum(update * update, axis=(1, 2))  3.4 us
  transfers between devices with their start and end apart: 6, of which 6 were waited for; matrix products, arithmetic and copies ran while one was open for 6% of the time, Pallas kernels for 0%

profile of v1, /device:TPU:0, one launch (start us, length us, event | category | flops | bytes accessed | tf_op | source)
XLA Modules:
  0.0 159.7 jit_solution(11186638025631292904)
XLA Ops:
  6.5 0.0 copy-start
  6.5 0.8 reshape.83
  7.4 0.8 reshape.82
  8.2 0.0 copy-done
  8.2 0.0 copy-start.3
  8.2 0.0 copy-start.4
  8.2 0.0 copy-start.2
  8.2 0.7 gather_fusion
  8.9 0.8 broadcast_select_fusion
  9.7 6.3 %all-to-all-start = ((bf16[4,16,2048]{2,1,0:T(8,128)(2,1)}), bf16[4,16,2048]{2,1,0:T(8,128)(2,1)S(1)}, u32[]{:S(2)}, u32[]{:S(2)}) async-start(bf16[4,16,2048]{2,1,0:T(8,128)(2,1)} %broadcast_select_fusion), calls=%async_computation | async-start | bytes 524288 | tf_op jit(solution)/shard_map/all_to_all | solution.py:36
  16.1 0.0 reduce-scatter.9.cloned.1.call-start
  16.1 0.6 broadcast.63
  16.7 0.0 copy-done.3
  16.7 0.7 reduce.6
  17.4 0.1 reshape.81
  17.5 0.6 broadcast.64
  18.1 0.0 copy-done.4
  18.1 0.7 reduce.7
  18.8 0.1 lt.36
  18.9 0.1 fusion.14
  19.0 6.0 %all-to-all-done = bf16[4,16,2048]{2,1,0:T(8,128)(2,1)S(1)} async-done(((bf16[4,16,2048]{2,1,0:T(8,128)(2,1)}), bf16[4,16,2048]{2,1,0:T(8,128)(2,1)S(1)}, u32[]{:S(2)}, u32[]{:S(2)}) %all-to-all-start) | async-done | bytes 262176 | tf_op jit(solution)/shard_map/all_to_all | solution.py:36
  25.0 0.1 fusion.12
  25.1 0.0 copy-done.2
  25.1 2.7 %fusion.1 = bf16[768,2048]{0,1:T(8,128)(2,1)} fusion(bf16[4,2,8,2048]{3,2,0,1:T(8,128)(2,1)S(1)} %fusion.12, bf16[4,2,8,768]{3,2,1,0:T(8,128)(2,1)S(1)} %bitcast.43), kind=kOutput, calls=%fused_computation.4 | convolution fusion | flops 102236160 | bytes 3325952 | tf_op jit(solution)/shard_map/dot_general | solution.py:51
  27.9 4.8 %copy.38 = bf16[768,2048]{1,0:T(8,128)(2,1)} copy(bf16[768,2048]{0,1:T(8,128)(2,1)} %fusion.1) | data formatting | bytes 6291456
  32.6 0.0 reduce-scatter.9.cloned.1.call-update
  32.6 0.0 reduce-scatter.7.cloned.1.call-start
  32.7 2.7 %fusion = bf16[768,2048]{0,1:T(8,128)(2,1)} fusion(bf16[4,2,8,2048]{3,2,0,1:T(8,128)(2,1)S(1)} %fusion.12, bf16[4,2,8,768]{3,2,1,0:T(8,128)(2,1)S(1)} %bitcast.44), kind=kOutput, calls=%fused_computation.3 | convolution fusion | flops 102236160 | bytes 3325952 | tf_op jit(solution)/shard_map/dot_general | solution.py:51
  35.4 4.7 %copy.36 = bf16[768,2048]{1,0:T(8,128)(2,1)} copy(bf16[768,2048]{0,1:T(8,128)(2,1)} %fusion) | data formatting | bytes 6291456
  40.2 0.0 copy-start.1
  40.2 0.0 reduce-scatter.7.cloned.1.call-update
  40.2 37.7 %reduce-scatter.9.cloned.1.call-done = bf16[96,2048]{1,0:T(8,128)(2,1)} async-done(((bf16[768,2048]{1,0:T(8,128)(2,1)}), bf16[96,2048]{1,0:T(8,128)(2,1)}) %reduce-scatter.9.cloned.1.call-update) | async-done | bytes 393232 | tf_op jit(solution)/shard_map/reduce_scatter | solution.py:53
  77.9 49.5 %reduce-scatter.7.cloned.1.call-done = bf16[96,2048]{1,0:T(8,128)(2,1)} async-done(((bf16[768,2048]{1,0:T(8,128)(2,1)}), bf16[96,2048]{1,0:T(8,128)(2,1)}) %reduce-scatter.7.cloned.1.call-update) | async-done | bytes 393232 | tf_op jit(solution)/shard_map/reduce_scatter | solution.py:53
  127.4 0.0 copy-done.1
  127.4 3.4 %multiply_reduce_fusion = (f32[2]{0:T(128)S(1)}, f32[2,96,2048]{2,1,0:T(8,128)S(1)}, f32[2]{0:T(128)S(1)}) fusion(bf16[2,96,2048]{2,1,0:T(8,128)(2,1)S(1)} %copy-done.1, bf16[2,96,2048]{2,1,0:T(8,128)(2,1)} %param.15, bf16[1,96,2048]{2,1,0:T(8,128)(2,1)} %bitcast.41, bf16[1,96,2048]{2,1,0:T(8,128)(2,1)} %bitcast.42, bf16[2,96,2048]{2,1,0:T(8,128)(2,1)} %param.14), kind=kLoop, calls=%fused_computation.20 | loop fusion | flops 8650748 | bytes 4718608 | tf_op jit(solution)/shard_map/reduce_sum | solution.py:66
  130.8 12.5 %psum.7 = f32[2]{0:T(128)S(1)} all-reduce(f32[2]{0:T(128)S(1)} %get-tuple-element.7), channel_id=1, replica_groups=mesh['expert'=4,'dp'=8] {'dp'}, use_global_device_ids=true, to_apply=%region_1.0 | all-reduce | flops 2 | bytes 16 | tf_op jit(solution)/shard_map/psum | solution.py:32
  143.3 0.1 collective-permute-start
  143.4 1.1 collective-permute-done
  144.5 0.0 collective-permute-start.1
  144.5 3.6 %collective-permute-done.1 = f32[2]{0:T(128)S(1)} collective-permute-done((f32[2]{0:T(128)S(1)}, f32[2]{0:T(128)S(1)}, u32[]{:S(2)}, u32[]{:S(2)}) %collective-permute-start.1) | collective-permute-done | bytes 40 | tf_op jit(solution)/shard_map/ppermute | solution.py:18
  148.1 1.4 collective-permute-start.2
  149.5 2.1 %collective-permute-done.2 = f32[2]{0:T(128)S(1)} collective-permute-done((f32[2]{0:T(128)S(1)}, f32[2]{0:T(128)S(1)}, u32[]{:S(2)}, u32[]{:S(2)}) %collective-permute-start.2) | collective-permute-done | bytes 40 | tf_op jit(solution)/shard_map/ppermute | solution.py:18
  151.7 1.2 fusion.7
  (7 shorter events, 0.0 us)
Async XLA Ops:
  6.5 1.6 %copy-start = (bf16[128,2048]{1,0:T(8,128)(2,1)S(1)}, bf16[128,2048]{1,0:T(8,128)(2,1)}, u32[]{:S(2)}) copy-start(bf16[128,2048]{1,0:T(8,128)(2,1)} %param.8) | copy-start | bytes 1572868
  8.2 8.5 %copy-start.3 = (f32[1,64]{1,0:T(1,128)S(1)}, f32[1,64]{1,0:T(1,128)}, u32[]{:S(2)}) copy-start(f32[1,64]{1,0:T(1,128)} %param.11) | copy-start | bytes 772
  8.2 9.9 %copy-start.4 = (s32[1,8]{1,0:T(1,128)S(1)}, s32[1,8]{1,0:T(1,128)}, u32[]{:S(2)}) copy-start(s32[1,8]{1,0:T(1,128)} %param.12) | copy-start | bytes 100
  8.2 16.9 %copy-start.2 = (bf16[64,768]{1,0:T(8,128)(2,1)S(1)}, bf16[64,768]{1,0:T(8,128)(2,1)}, u32[]{:S(2)}) copy-start(bf16[64,768]{1,0:T(8,128)(2,1)} %param.10) | copy-start | bytes 294916
  9.7 15.3 %all-to-all-start = ((bf16[4,16,2048]{2,1,0:T(8,128)(2,1)}), bf16[4,16,2048]{2,1,0:T(8,128)(2,1)S(1)}, u32[]{:S(2)}, u32[]{:S(2)}) async-start(bf16[4,16,2048]{2,1,0:T(8,128)(2,1)} %broadcast_select_fusion), calls=%async_computation | async-start | bytes 524288 | tf_op jit(solution)/shard_map/all_to_all | solution.py:36
  16.1 61.8 %reduce-scatter.9.cloned.1.call-start = ((), (), s32[]{:S(2)}) async-start(), calls=%async_computation.4 | async-start | bytes 3538944 | tf_op jit(solution)/shard_map/reduce_scatter | solution.py:53
  32.6 94.7 %reduce-scatter.7.cloned.1.call-start = ((), (), s32[]{:S(2)}) async-start(), calls=%async_computation.3 | async-start | bytes 3538944 | tf_op jit(solution)/shard_map/reduce_scatter | solution.py:53
  40.2 87.2 %copy-start.1 = (bf16[2,96,2048]{2,1,0:T(8,128)(2,1)S(1)}, bf16[2,96,2048]{2,1,0:T(8,128)(2,1)}, u32[]{:S(2)}) copy-start(bf16[2,96,2048]{2,1,0:T(8,128)(2,1)} %param.13) | copy-start | bytes 2359300
  143.3 1.2 collective-permute-start
  144.5 3.6 %collective-permute-start.1 = (f32[2]{0:T(128)S(1)}, f32[2]{0:T(128)S(1)}, u32[]{:S(2)}, u32[]{:S(2)}) collective-permute-start(f32[2]{0:T(128)S(1)} %add.64), channel_id=1, source_target_pairs={{0,2},{1,3},{2,0},{3,1},{4,6},{5,7},{6,4},{7,5},{8,10},{9,11},{10,... | collective-permute-start | bytes 32 | tf_op jit(solution)/shard_map/ppermute | solution.py:18
  148.1 3.6 %collective-permute-start.2 = (f32[2]{0:T(128)S(1)}, f32[2]{0:T(128)S(1)}, u32[]{:S(2)}, u32[]{:S(2)}) collective-permute-start(f32[2]{0:T(128)S(1)} %add.65), channel_id=1, source_target_pairs={{0,4},{1,5},{2,6},{3,7},{4,0},{5,1},{6,2},{7,3},{8,12},{9,13},{10,... | collective-permute-start | bytes 32 | tf_op jit(solution)/shard_map/ppermute | solution.py:18
Sparse Core Ops, SparseCore 0:
  32.8 45.1 reduce-scatter.8
  81.3 46.0 reduce-scatter.6
